TPU v7x, 32 devices: a whole 2x2x4 slice. The times are simulated.
32 devices in a mesh: aux: 4 (over z), pair: 8 (over y, x, core).
Axes of the slice: x: 2, y: 2, z: 4, core: 2. Of those that a mesh axis runs over, the one named last changes fastest.
Arguments:
- b_three: bfloat16 [4096, 2048], P('pair', 'aux'), may hold values from -0.13183594 to 0.13183594
- metric: bfloat16 [2048, 2048], P(None, 'aux'), may hold values from -1 to 2
- aux_map: int32 [64, 32], P('pair', 'aux'), may hold values 0 or 1
- domains: int32 [80, 4], replicated, may hold values from 0 to 63, as said below
- counts: int32 [80], P('pair'), may hold values from 1 to 4, as said below
Outputs:
- pair_integrals: float32 [80, 256, 256], P('pair', 'aux')
Inputs may be any that keep to these rules, and one draw needn't show every extreme that they name: `domains`: of the 40 slots of the pairs of one index of pair (pairs q * 10 to (q + 1) * 10 - 1), at most 5 name blocks held by one index of pair (blocks o * 8 to (o + 1) * 8 - 1), and exactly 5 for some such index in every draw. `counts`: slots at or past a pair's count are padding.
All inputs are finite; a program needn't handle non-finite values. No bound on the sum of `aux_map` on one device may be relied on, other than what follows from the above.
Results may differ from a plain program's by a relative error of at most 0.00079.
Values may be sent and summed in bfloat16 or wider, within the bound.
A program may use at most 64 MiB of HBM per device.

v0:
```python
import jax
import jax.numpy as jnp
from jax import lax
from jax.sharding import PartitionSpec as P


def per_device(b_three, metric, aux_map, domains, counts):
    rows_dev, aux_dev = b_three.shape
    blocks_dev, aux_blocks = aux_map.shape
    width_cw = rows_dev // blocks_dev
    aux_width = aux_dev // aux_blocks
    keep_mask = aux_map.astype(jnp.bfloat16)
    masked = (
        b_three.reshape(blocks_dev, width_cw, aux_blocks, aux_width) * keep_mask[:, None, :, None]
    ).reshape(rows_dev, aux_dev)
    fitted = jnp.dot(
        lax.all_gather(masked, "aux", axis=1, tiled=True),
        metric,
        preferred_element_type=jnp.float32,
    ).astype(jnp.bfloat16)
    block_table = fitted.reshape(blocks_dev, width_cw * aux_dev)
    peer_count = lax.axis_size("pair")
    own_index = lax.axis_index("pair")
    pairs_dev = counts.shape[0]
    domain_max = domains.shape[1]
    slot_count = pairs_dev * domain_max
    all_domains = domains.reshape(peer_count, slot_count)
    own_domains = lax.dynamic_slice_in_dim(all_domains, own_index, 1, 0)[0]
    shard_piece = lax.all_gather(block_table, "pair", axis=0, tiled=True)
    block_ids = jnp.arange(shard_piece.shape[0], dtype=jnp.int32)
    onehot = (own_domains[:, None] == block_ids[None, :]).astype(jnp.bfloat16)
    chosen = jnp.dot(onehot, shard_piece, preferred_element_type=jnp.float32).astype(jnp.bfloat16)
    stacks = chosen.reshape(pairs_dev, domain_max * width_cw, aux_dev)
    partial_value = jnp.einsum("pax,pbx->pab", stacks, stacks, preferred_element_type=jnp.float32)
    slot_of = jnp.arange(domain_max * width_cw, dtype=jnp.int32) // width_cw
    live_rows = slot_of[None, :] < counts[:, None]
    partial_value = jnp.where(
        live_rows[:, :, None] & live_rows[:, None, :], partial_value, jnp.zeros_like(partial_value)
    )
    return lax.psum_scatter(partial_value, "aux", scatter_dimension=1, tiled=True)


def solution(mesh):
    return jax.shard_map(
        per_device,
        mesh=mesh,
        in_specs=(P("pair", "aux"), P(None, "aux"), P("pair", "aux"), P(), P("pair")),
        out_specs=P("pair", "aux", None),
        check_vma=False,
    )
```

profile of v0, /device:TPU:1, one launch (start us, length us, event | category | flops | bytes accessed | tf_op | source)
XLA Modules:
  0.0 171.9 jit_solution(9193353961309677917)
XLA Ops:
  6.5 0.0 copy-start
  6.5 0.0 all-gather.3.cloned.1.call-start
  6.5 0.8 convert_element_type.10
  7.4 0.2 mul.11
  7.6 1.4 mul.12
  9.0 2.1 %mul.13 = bf16[512,512]{1,0:T(8,128)(2,1)} multiply(bf16[512,512]{1,0:T(8,128)(2,1)} %param.5, bf16[512,512]{1,0:T(8,128)(2,1)} %mul.12) | non-fusion elementwise | flops 262144 | bytes 1572864 | tf_op jit(solution)/shard_map/mul | solution.py:14
  11.1 0.0 all-gather.3.cloned.1.call-update
  11.1 0.0 copy-start.1
  11.2 0.0 copy-start.2
  11.2 0.0 all-gather.5.cloned.1.call-start
  11.2 47.6 %all-gather.3.cloned.1.call-done = bf16[512,2048]{1,0:T(8,128)(2,1)} async-done(((bf16[512,512]{1,0:T(8,128)(2,1)}), bf16[512,2048]{1,0:T(8,128)(2,1)}) %all-gather.3.cloned.1.call-update) | async-done | bytes 2097168 | tf_op jit(solution)/shard_map/all_gather | solution.py:17
  58.9 2.8 %convolution_convert_fusion.1 = bf16[512,512]{1,0:T(8,128)(2,1)S(1)} fusion(bf16[512,2048]{1,0:T(8,128)(2,1)} %all-gather.3.cloned.1.call-done, bf16[2048,512]{1,0:T(8,128)(2,1)S(1)} %copy-done), kind=kOutput, calls=%fused_computation.2 | convolution fusion | flops 1074003968 | bytes 4718592 | tf_op jit(solution)/shard_map/dot_general | solution.py:16
  61.7 1.0 reshape.77
  62.7 0.0 all-gather.5.cloned.1.call-update
  62.8 0.0 reduce-scatter.2.cloned.1.call-start
  62.8 0.1 copy.6
  62.9 0.1 reshape.76
  63.0 0.1 broadcast_compare_fusion
  63.1 35.8 %all-gather.5.cloned.1.call-done = bf16[64,32768]{1,0:T(8,128)(2,1)} async-done(((bf16[8,32768]{1,0:T(8,128)(2,1)}), bf16[64,32768]{1,0:T(8,128)(2,1)}) %all-gather.5.cloned.1.call-update) | async-done | bytes 4194320 | tf_op jit(solution)/shard_map/all_gather | solution.py:29
  98.9 4.6 %convolution_convert_fusion = bf16[40,32768]{1,0:T(8,128)(2,1)} fusion(bf16[64,32768]{1,0:T(8,128)(2,1)} %all-gather.5.cloned.1.call-done, s32[40]{0:T(128)S(1)} %dynamic-slice_bitcast_fusion), kind=kOutput, calls=%fused_computation | convolution fusion | flops 169085440 | bytes 6815904 | tf_op jit(solution)/shard_map/dot_general | solution.py:32
  103.5 5.3 %reshape.78 = bf16[10,256,512]{2,1,0:T(8,128)(2,1)} reshape(bf16[40,32768]{1,0:T(8,128)(2,1)} %convolution_convert_fusion) | data formatting | bytes 5242880 | tf_op jit(solution)/shard_map/reshape | solution.py:33
  108.8 5.0 %and_select_fusion = f32[10,256,256]{2,1,0:T(8,128)} fusion(bf16[10,256,512]{2,1,0:T(8,128)(2,1)} %reshape.78, pred[10,256]{1,0:T(8,128)(4,1)S(1)} %broadcast_compare_fusion), kind=kOutput, calls=%fused_computation.1 | convolution fusion | flops 672399360 | bytes 5245440 | tf_op jit(solution)/shard_map/pax,pbx->pab/dot_general | solution.py:34
  113.7 0.0 reduce-scatter.2.cloned.1.call-update
  113.8 51.6 %reduce-scatter.2.cloned.1.call-done = f32[10,64,256]{2,1,0:T(8,128)} async-done(((f32[10,256,256]{2,1,0:T(8,128)}), f32[10,64,256]{2,1,0:T(8,128)}) %reduce-scatter.2.cloned.1.call-update) | async-done | bytes 655376 | tf_op jit(solution)/shard_map/reduce_scatter | solution.py:40
  (5 shorter events, 0.0 us)
Async XLA Ops:
  6.5 52.3 %copy-start = (bf16[2048,512]{1,0:T(8,128)(2,1)S(1)}, bf16[2048,512]{1,0:T(8,128)(2,1)}, u32[]{:S(2)}) copy-start(bf16[2048,512]{1,0:T(8,128)(2,1)} %param.6) | copy-start | bytes 6291460
  6.5 52.3 %all-gather.3.cloned.1.call-start = ((), (), s32[]{:S(2)}) async-start(), calls=%async_computation.1 | async-start | bytes 2621440 | tf_op jit(solution)/shard_map/all_gather | solution.py:17
  11.1 51.7 %copy-start.1 = (s32[80,4]{0,1:T(4,128)S(1)}, s32[80,4]{0,1:T(4,128)}, u32[]{:S(2)}) copy-start(s32[80,4]{0,1:T(4,128)} %param.8) | copy-start | bytes 3844
  11.2 51.9 %copy-start.2 = (s32[10]{0:T(128)S(1)}, s32[10]{0:T(128)}, u32[]{:S(2)}) copy-start(s32[10]{0:T(128)} %param.9) | copy-start | bytes 124
  11.2 87.7 %all-gather.5.cloned.1.call-start = ((), (), s32[]{:S(2)}) async-start(), calls=%async_computation.2 | async-start | bytes 4718592 | tf_op jit(solution)/shard_map/all_gather | solution.py:29
  62.8 102.6 %reduce-scatter.2.cloned.1.call-start = ((), (), s32[]{:S(2)}) async-start(), calls=%async_computation.3 | async-start | bytes 3276800 | tf_op jit(solution)/shard_map/reduce_scatter | solution.py:40
Sparse Core Ops, SparseCore 0:
  11.3 47.5 all-gather.2
  62.9 35.9 all-gather.4
  113.9 51.4 reduce-scatter.1
where the time goes:
time: 173 us; the launch traced here: 172 us
  waiting for transfers between devices  135 us (78%)
  between operations  13.2 us (8%)
  matrix products  12.4 us (7%)
  local copies, waits for them, and re-layouts  8.12 us (5%)
  other arithmetic  3.04 us (2%)
    reduce_scatter x1, waiting for transfers between devices, per_device(): lax.psum_scatter(partial_value, 'aux', scatter_dimension=1, tiled=True)  51.6 us
    all_gather x1, waiting for transfers between devices, per_device(): lax.all_gather(masked, 'aux', axis=1, tiled=True)  47.6 us
    all_gather x1, waiting for transfers between devices, per_device(): shard_piece = lax.all_gather(block_table, 'pair', axis=0, tiled=True)  35.8 us
    reshape x1, local copies, waits for them, and re-layouts, per_device(): stacks = chosen.reshape(pairs_dev, domain_max * width_cw, aux_dev)  5.27 us
    dot_general x1, matrix products, per_device(): jnp.einsum('pax,pbx->pab', stacks, stacks, preferred_element_type=jnp.flo...  4.97 us
    dot_general x1, matrix products, per_device(): jnp.dot(onehot, shard_piece, preferred_element_type=jnp.float32)  4.62 us
  transfers between devices with their start and end apart: 3, of which 3 were waited for; matrix products, arithmetic and copies ran while one was open for 0% of the time, Pallas kernels for 0%

commit v1 on v0

v1 whole, which is shorter than its diff:
```python
import functools

import jax
import jax.numpy as jnp
from jax import lax
from jax.experimental import pallas as pl
from jax.experimental.pallas import tpu as pltpu
from jax.sharding import PartitionSpec as P

MESH = pl.DeviceIdType.MESH


def kernel(n, n_pair, b_ref, metric_ref, dom_ref, cnt_ref, out_ref,
           b_all, table, g_send, g_recv, d_own, d_recv,
           r_s, r_r, l_s, l_r, p_s, p_r, f_s, f_r, g_s, g_r, d_s, d_r):
    chunks, rows, depth = b_ref.shape
    pairs, slab, width = out_ref.shape
    slots = dom_ref.shape[1]
    chips = n_pair // 2
    z = lax.axis_index("aux")
    q = lax.axis_index("pair")
    core = lax.rem(q, 2)
    chip = q // 2
    partner = q + 1 - 2 * core
    has_right = z + 1 < n
    has_left = z > 0

    def chip_at(k):
        return lax.rem(chip + k + chips, chips) * 2 + core

    barrier = pltpu.get_barrier_semaphore()
    for k in range(1, n):
        pl.semaphore_signal(barrier, inc=1, device_id=(lax.rem(z + k, n), q), device_id_type=MESH)
    for k in range(1, chips):
        pl.semaphore_signal(barrier, inc=1, device_id=(z, chip_at(k)), device_id_type=MESH)
    pl.semaphore_signal(barrier, inc=1, device_id=(z, partner), device_id_type=MESH)
    pl.semaphore_wait(barrier, n + chips - 1)

    def remote(src, dst, send, recv, device):
        return pltpu.make_async_remote_copy(
            src_ref=src, dst_ref=dst, send_sem=send, recv_sem=recv, device_id=device, device_id_type=MESH)

    def along(h, c, right):
        step = 1 if right else -1
        origin = z - step * h
        send, recv = (r_s, r_r) if right else (l_s, l_r)
        src = b_ref.at[c] if h == 0 else b_all.at[origin, c]
        return remote(src, b_all.at[origin, c], send.at[h, c], recv.at[h, c], (z + step, q))

    def arrival(h, c, right):
        recv = r_r if right else l_r
        origin = z - 1 - h if right else z + 1 + h
        return remote(b_ref.at[c], b_all.at[origin, c], recv.at[h, c], recv.at[h, c], (z, partner))

    def own_chunk(c):
        for right in (True, False):
            @pl.when(has_right if right else has_left)
            def _():
                along(0, c, right).start()

    def relay(h, c):
        for right in (True, False):
            came = z - h >= 0 if right else z + h < n

            @pl.when(came)
            def _():
                arrival(h - 1, c, right).wait_recv()

                if h < n - 1:
                    @pl.when(has_right if right else has_left)
                    def _():
                        along(h, c, right).start()

    def spread(k, c):
        target = partner if k == 0 else chip_at(k)
        return remote(table.at[q, c], table.at[q, c], p_s.at[k, c], p_r.at[k, c], (z, target))

    def forward(k, c):
        origin = chip_at(-k)
        return remote(table.at[origin, c], table.at[origin, c], f_s.at[k, c], f_r.at[k, c], (z, partner))

    def fit(c):
        total = jnp.dot(b_ref[c], metric_ref[pl.ds(pl.multiple_of(z * depth, depth), depth), :],
                        preferred_element_type=jnp.float32)
        for k in range(1, n):
            origin = lax.rem(z + k, n)
            total += jnp.dot(b_all[origin, c],
                             metric_ref[pl.ds(pl.multiple_of(origin * depth, depth), depth), :],
                             preferred_element_type=jnp.float32)
        table[q, c] = total.astype(table.dtype)
        for k in list(range(1, chips)) + [0]:
            spread(k, c).start()

    def pass_on(c):
        for k in range(1, chips):
            spread_in = remote(table.at[chip_at(-k), c], table.at[chip_at(-k), c],
                               p_s.at[k, c], p_r.at[k, c], (z, partner))
            spread_in.wait_recv()
            forward(k, c).start()

    own_chunk(0)

    def stage(step, carry):
        @pl.when(step + 1 < chunks)
        def _():
            own_chunk(step + 1)
        for h in range(1, n):
            @pl.when((step + 1 >= h) & (step + 1 - h < chunks))
            def _():
                relay(h, step + 1 - h)

        @pl.when((step + 2 >= n) & (step + 2 - n < chunks))
        def _():
            fit(step + 2 - n)

        @pl.when((step >= n) & (step - n < chunks))
        def _():
            pass_on(step - n)
        return carry

    lax.fori_loop(0, chunks + n, stage, 0)

    def finish(c, carry):
        remote(table.at[partner, c], table.at[partner, c], p_s.at[0, c], p_r.at[0, c],
               (z, partner)).wait_recv()
        for k in range(1, chips):
            origin = chip_at(-k) + 1 - 2 * core
            remote(table.at[origin, c], table.at[origin, c], f_s.at[k, c], f_r.at[k, c],
                   (z, partner)).wait_recv()
        return carry

    lax.fori_loop(0, chunks, finish, 0)

    row_of = lax.broadcasted_iota(jnp.int32, (width, width), 0)
    col_of = lax.broadcasted_iota(jnp.int32, (width, width), 1)

    def gram_copy(k, p):
        return remote(g_send.at[lax.rem(z + k, n), p], g_recv.at[k - 1, p],
                      g_s.at[k - 1, p], g_r.at[k - 1, p], (lax.rem(z + k, n), q))

    def gram(p, carry):
        blocks = []
        for s in range(slots):
            name = dom_ref[q * pairs + p, s]
            blocks.append(table[name // chunks, lax.rem(name, chunks)])
        stack = jnp.concatenate(blocks, axis=0)
        full = lax.dot_general(stack, stack, (((1,), (1,)), ((), ())), preferred_element_type=jnp.float32)
        d_own[p] = jnp.sum(jnp.where(row_of == col_of, full, 0.0), axis=0, keepdims=True)
        for d in range(n):
            part = full[d * slab:(d + 1) * slab]

            @pl.when(z == d)
            def _():
                out_ref[p] = part

            @pl.when(z != d)
            def _():
                g_send[d, p] = part.astype(g_send.dtype)
        for k in range(1, n):
            gram_copy(k, p).start()
        return carry

    lax.fori_loop(0, pairs, gram, 0)

    def diag_copy(k):
        return remote(d_own, d_recv.at[k - 1], d_s.at[k - 1], d_r.at[k - 1], (lax.rem(z + k, n), q))

    for k in range(1, n):
        diag_copy(k).start()

    def add(p, carry):
        total = out_ref[p]
        for k in range(1, n):
            gram_copy(k, p).wait_recv()
            total += g_recv[k - 1, p].astype(jnp.float32)
        out_ref[p] = total
        return carry

    lax.fori_loop(0, pairs, add, 0)
    for k in range(1, n):
        diag_copy(k).wait_recv()

    slab_row = lax.broadcasted_iota(jnp.int32, (slab, width), 0) + z * slab
    slab_col = lax.broadcasted_iota(jnp.int32, (slab, width), 1)
    last = jnp.maximum(slab_row, slab_col)

    def close(p, carry):
        diag = d_own[p]
        for k in range(1, n):
            diag += d_recv[k - 1, p]
        value = jnp.where(slab_row == slab_col, diag, out_ref[p])
        out_ref[p] = jnp.where(last < cnt_ref[p] * rows, value, 0.0)
        return carry

    lax.fori_loop(0, pairs, close, 0)

    def drain(c, carry):
        for right in (True, False):
            for h in range(n - 1):
                goes = (has_right & (z - h >= 0)) if right else (has_left & (z + h < n))

                @pl.when(goes)
                def _():
                    along(h, c, right).wait_send()
        for k in range(chips):
            spread(k, c).wait_send()
        for k in range(1, chips):
            forward(k, c).wait_send()
        return carry

    lax.fori_loop(0, chunks, drain, 0)

    def drain_gram(p, carry):
        for k in range(1, n):
            gram_copy(k, p).wait_send()
        return carry

    lax.fori_loop(0, pairs, drain_gram, 0)
    for k in range(1, n):
        diag_copy(k).wait_send()


def per_device(n, n_pair, b_three, metric, aux_map, domains, counts):
    rows_dev, aux_dev = b_three.shape
    blocks_dev, aux_blocks = aux_map.shape
    width_cw = rows_dev // blocks_dev
    aux_width = aux_dev // aux_blocks
    pairs = counts.shape[0]
    slots = domains.shape[1]
    width = slots * width_cw
    slab = width // n
    columns = metric.shape[1]
    chips = n_pair // 2
    mask = jnp.repeat(aux_map.astype(jnp.bfloat16), aux_width, axis=1)
    masked = b_three.reshape(blocks_dev, width_cw, aux_dev) * mask[:, None, :]
    vmem = pl.BlockSpec(memory_space=pltpu.VMEM)
    smem = pl.BlockSpec(memory_space=pltpu.SMEM)
    dma = pltpu.SemaphoreType.DMA
    return pl.pallas_call(
        functools.partial(kernel, n, n_pair),
        out_shape=jax.ShapeDtypeStruct((pairs, slab, width), jnp.float32),
        in_specs=[vmem, vmem, smem, smem],
        out_specs=vmem,
        scratch_shapes=[
            pltpu.VMEM((n, blocks_dev, width_cw, aux_dev), jnp.bfloat16),
            pltpu.VMEM((n_pair, blocks_dev, width_cw, columns), jnp.bfloat16),
            pltpu.VMEM((n, pairs, slab, width), jnp.bfloat16),
            pltpu.VMEM((n - 1, pairs, slab, width), jnp.bfloat16),
            pltpu.VMEM((pairs, 1, width), jnp.float32),
            pltpu.VMEM((n - 1, pairs, 1, width), jnp.float32),
            dma((n - 1, blocks_dev)), dma((n - 1, blocks_dev)),
            dma((n - 1, blocks_dev)), dma((n - 1, blocks_dev)),
            dma((chips, blocks_dev)), dma((chips, blocks_dev)),
            dma((chips, blocks_dev)), dma((chips, blocks_dev)),
            dma((n - 1, pairs)), dma((n - 1, pairs)),
            dma((n - 1,)), dma((n - 1,)),
        ],
        compiler_params=pltpu.CompilerParams(
            collective_id=0, has_side_effects=True, vmem_limit_bytes=60 * 1024 * 1024),
    )(masked, metric, domains, counts)


def solution(mesh):
    return jax.shard_map(
        functools.partial(per_device, mesh.shape["aux"], mesh.shape["pair"]),
        mesh=mesh,
        in_specs=(P("pair", "aux"), P(None, "aux"), P("pair", "aux"), P(), P("pair")),
        out_specs=P("pair", "aux", None),
        check_vma=False,
    )
```

time: 173 us -> 86.7 us (0.50)
  waiting for transfers between devices: 135 us -> 0 us
  Pallas kernels: 0 us -> 80.3 us
  between operations: 13.2 us -> 0.01 us
  matrix products: 12.4 us -> 0 us
  local copies, waits for them, and re-layouts: 8.12 us -> 3.53 us
    all_gather x2 -> x0, waiting for transfers between devices: 83.4 us -> none  [the longest x1 47.6 us: per_device(): lax.all_gather(masked, 'aux', axis=1, tiled=True)]
    pallas_call x0 -> x1, Pallas kernels: none -> 80.3 us  [per_device(): pl.pallas_call(functools.partial(kernel, n, n_pair), out_shape=jax.ShapeD...]
    reduce_scatter x1 -> x0, waiting for transfers between devices: 51.6 us -> none  [per_device(): lax.psum_scatter(partial_value, 'aux', scatter_dimension=1, tiled=True)]
    dot_general x3 -> x0, matrix products: 12.4 us -> none  [the longest x1 4.97 us: per_device(): jnp.einsum('pax,pbx->pab', stacks, stacks, preferred_element_type=jnp.flo...]
    reshape x3 -> x0, local copies, waits for them, and re-layouts: 6.38 us -> none  [the longest x1 5.27 us: per_device(): stacks = chosen.reshape(pairs_dev, domain_max * width_cw, aux_dev)]
    unnamed x7 -> x2, local copies, waits for them, and re-layouts: 0.12 us -> 3.36 us
  transfers between devices with their start and end apart: 3 -> 0, of which waited for: 3 -> 0; matrix products, arithmetic and copies ran while one was open for 0% -> 0% of each run, Pallas kernels for 0% -> 0%
where the time goes in v1:
time: 86.7 us; the launch traced here: 86.4 us
  Pallas kernels  80.3 us (93%)
  local copies, waits for them, and re-layouts  3.53 us (4%)
  other arithmetic  2.56 us (3%)
    pallas_call x1, Pallas kernels, per_device(): pl.pallas_call(functools.partial(kernel, n, n_pair), out_shape=jax.ShapeD...  80.3 us
    unnamed x2, local copies, waits for them, and re-layouts  3.36 us
    mul x1, other arithmetic, per_device(): masked = b_three.reshape(blocks_dev, width_cw, aux_dev) * mask[:, None, :]  1.87 us

profile of v1, /device:TPU:1, one launch (start us, length us, event | category | flops | bytes accessed | tf_op | source)
XLA Modules:
  0.0 86.4 jit_solution(5279079636255007474)
XLA Ops:
  0.0 0.7 convert_element_type.3
  0.7 0.1 broadcast_in_dim.3
  0.8 0.1 mul.10
  0.9 1.4 %copy.6.dom_ref = s32[80,4]{1,0:T(8,128)} copy(s32[80,4]{0,1:T(4,128)} %param.8) | data formatting | bytes 2560 | tf_op args[3]
  2.3 1.9 %broadcast_multiply_fusion.b_ref = bf16[8,64,512]{2,1,0:T(8,128)(2,1)} fusion(bf16[8,64,512]{2,1,0:T(8,128)(2,1)} %bitcast.1, bf16[8,512]{1,0:T(8,128)(2,1)S(1)} %mul.10), kind=kLoop, calls=%fused_computation | loop fusion | flops 262144 | bytes 1056768 | tf_op jit(solution)/shard_map/mul | solution.py:235
  4.1 80.3 %shard_map.55 = f32[10,64,256]{2,1,0:T(8,128)} custom-call(bf16[8,64,512]{2,1,0:T(8,128)(2,1)} %broadcast_multiply_fusion.b_ref, bf16[2048,512]{1,0:T(8,128)(2,1)} %metric_ref.1, s32[80,4]{1,0:T(8,128)} %copy.6.dom_ref, s32[10]{0:T(128)} %cnt_ref.1), custom_call_target="tpu_custom_call" | custom-call | tf_op jit(solution)/shard_map/pallas_call | solution.py:239
  84.4 2.0 %copy.8 = f32[10,64,256]{2,1,0:T(8,128)} copy(f32[10,64,256]{2,1,0:T(8,128)} %shard_map.55) | data formatting | bytes 1310720

commit v2 on v1

--- a/solution.py
+++ b/solution.py
@@ -10,12 +10,12 @@
 MESH = pl.DeviceIdType.MESH
 
 
-def kernel(n, n_pair, b_ref, metric_ref, dom_ref, cnt_ref, out_ref,
-           b_all, table, g_send, g_recv, d_own, d_recv,
+def kernel(n, n_pair, b_hbm, metric_hbm, map_ref, dom_ref, out_ref, diag_ref,
+           b_raw, b_ref, metric_ref, in_sem, b_all, table, g_send, g_recv, d_own, d_recv,
            r_s, r_r, l_s, l_r, p_s, p_r, f_s, f_r, g_s, g_r, d_s, d_r):
-    chunks, rows, depth = b_ref.shape
+    chunks, rows, depth = b_hbm.shape
     pairs, slab, width = out_ref.shape
-    slots = dom_ref.shape[1]
+    slots = dom_ref.shape[0]
     chips = n_pair // 2
     z = lax.axis_index("aux")
     q = lax.axis_index("pair")
@@ -28,12 +28,24 @@
     def chip_at(k):
         return lax.rem(chip + k + chips, chips) * 2 + core
 
+    load_b = pltpu.make_async_copy(b_hbm, b_raw, in_sem.at[0])
+    load_metric = pltpu.make_async_copy(metric_hbm, metric_ref, in_sem.at[1])
+    load_b.start()
+    load_metric.start()
     barrier = pltpu.get_barrier_semaphore()
     for k in range(1, n):
         pl.semaphore_signal(barrier, inc=1, device_id=(lax.rem(z + k, n), q), device_id_type=MESH)
     for k in range(1, chips):
         pl.semaphore_signal(barrier, inc=1, device_id=(z, chip_at(k)), device_id_type=MESH)
     pl.semaphore_signal(barrier, inc=1, device_id=(z, partner), device_id_type=MESH)
+    aux_blocks = map_ref.shape[1]
+    spread_row = lax.broadcasted_iota(jnp.int32, (aux_blocks, depth), 0)
+    spread_col = lax.broadcasted_iota(jnp.int32, (aux_blocks, depth), 1) // (depth // aux_blocks)
+    keep = jnp.dot(map_ref[...].astype(jnp.float32), (spread_row == spread_col).astype(jnp.float32),
+                   preferred_element_type=jnp.float32)
+    load_b.wait()
+    for c in range(chunks):
+        b_ref[c] = (b_raw[c].astype(jnp.float32) * keep[c:c + 1, :]).astype(b_ref.dtype)
     pl.semaphore_wait(barrier, n + chips - 1)
 
     def remote(src, dst, send, recv, device):
@@ -99,6 +111,7 @@
             forward(k, c).start()
 
     own_chunk(0)
+    load_metric.wait()
 
     def stage(step, carry):
         @pl.when(step + 1 < chunks)
@@ -141,7 +154,7 @@
     def gram(p, carry):
         blocks = []
         for s in range(slots):
-            name = dom_ref[q * pairs + p, s]
+            name = dom_ref[s, q * pairs + p]
             blocks.append(table[name // chunks, lax.rem(name, chunks)])
         stack = jnp.concatenate(blocks, axis=0)
         full = lax.dot_general(stack, stack, (((1,), (1,)), ((), ())), preferred_element_type=jnp.float32)
@@ -180,19 +193,10 @@
     for k in range(1, n):
         diag_copy(k).wait_recv()
 
-    slab_row = lax.broadcasted_iota(jnp.int32, (slab, width), 0) + z * slab
-    slab_col = lax.broadcasted_iota(jnp.int32, (slab, width), 1)
-    last = jnp.maximum(slab_row, slab_col)
-
-    def close(p, carry):
-        diag = d_own[p]
-        for k in range(1, n):
-            diag += d_recv[k - 1, p]
-        value = jnp.where(slab_row == slab_col, diag, out_ref[p])
-        out_ref[p] = jnp.where(last < cnt_ref[p] * rows, value, 0.0)
-        return carry
-
-    lax.fori_loop(0, pairs, close, 0)
+    diag = d_own[...]
+    for k in range(1, n):
+        diag += d_recv[k - 1]
+    diag_ref[...] = diag
 
     def drain(c, carry):
         for right in (True, False):
@@ -220,28 +224,45 @@
         diag_copy(k).wait_send()
 
 
+def close_kernel(rows, total_ref, diag_ref, cnt_ref, out_ref):
+    pairs, slab, width = out_ref.shape
+    slab_row = lax.broadcasted_iota(jnp.int32, (slab, width), 0) + lax.axis_index("aux") * slab
+    slab_col = lax.broadcasted_iota(jnp.int32, (slab, width), 1)
+    last = jnp.maximum(slab_row, slab_col)
+
+    def close(p, carry):
+        value = jnp.where(slab_row == slab_col, diag_ref[p], total_ref[p])
+        out_ref[p] = jnp.where(last < cnt_ref[p] * rows, value, 0.0)
+        return carry
+
+    lax.fori_loop(0, pairs, close, 0)
+
+
 def per_device(n, n_pair, b_three, metric, aux_map, domains, counts):
     rows_dev, aux_dev = b_three.shape
     blocks_dev, aux_blocks = aux_map.shape
     width_cw = rows_dev // blocks_dev
-    aux_width = aux_dev // aux_blocks
     pairs = counts.shape[0]
     slots = domains.shape[1]
     width = slots * width_cw
     slab = width // n
     columns = metric.shape[1]
     chips = n_pair // 2
-    mask = jnp.repeat(aux_map.astype(jnp.bfloat16), aux_width, axis=1)
-    masked = b_three.reshape(blocks_dev, width_cw, aux_dev) * mask[:, None, :]
     vmem = pl.BlockSpec(memory_space=pltpu.VMEM)
     smem = pl.BlockSpec(memory_space=pltpu.SMEM)
     dma = pltpu.SemaphoreType.DMA
-    return pl.pallas_call(
+    hbm = pl.BlockSpec(memory_space=pl.ANY)
+    total, diag = pl.pallas_call(
         functools.partial(kernel, n, n_pair),
-        out_shape=jax.ShapeDtypeStruct((pairs, slab, width), jnp.float32),
-        in_specs=[vmem, vmem, smem, smem],
-        out_specs=vmem,
+        out_shape=(jax.ShapeDtypeStruct((pairs, slab, width), jnp.float32),
+                   jax.ShapeDtypeStruct((pairs, 1, width), jnp.float32)),
+        in_specs=[hbm, hbm, vmem, smem],
+        out_specs=(vmem, vmem),
         scratch_shapes=[
+            pltpu.VMEM((blocks_dev, width_cw, aux_dev), jnp.bfloat16),
+            pltpu.VMEM((blocks_dev, width_cw, aux_dev), jnp.bfloat16),
+            pltpu.VMEM(metric.shape, jnp.bfloat16),
+            dma((2,)),
             pltpu.VMEM((n, blocks_dev, width_cw, aux_dev), jnp.bfloat16),
             pltpu.VMEM((n_pair, blocks_dev, width_cw, columns), jnp.bfloat16),
             pltpu.VMEM((n, pairs, slab, width), jnp.bfloat16),
@@ -257,7 +278,13 @@
         ],
         compiler_params=pltpu.CompilerParams(
             collective_id=0, has_side_effects=True, vmem_limit_bytes=60 * 1024 * 1024),
-    )(masked, metric, domains, counts)
+    )(b_three.reshape(blocks_dev, width_cw, aux_dev), metric, aux_map, domains.T)
+    return pl.pallas_call(
+        functools.partial(close_kernel, width_cw),
+        out_shape=jax.ShapeDtypeStruct((pairs, slab, width), jnp.float32),
+        in_specs=[vmem, vmem, smem],
+        out_specs=vmem,
+    )(total, diag, counts)
 
 
 def solution(mesh):

time: 86.7 us -> 81.6 us (0.941)
  local copies, waits for them, and re-layouts: 3.53 us -> 0 us
  other arithmetic: 2.56 us -> 0 us
  Pallas kernels: 80.3 us -> 81.4 us
    unnamed x2 -> x0, local copies, waits for them, and re-layouts: 3.36 us -> none
    mul x1 -> x0, other arithmetic: 1.87 us -> none  [per_device(): masked = b_three.reshape(blocks_dev, width_cw, aux_dev) * mask[:, None, :]]
    pallas_call x1 -> x2, Pallas kernels: 80.3 us -> 81.4 us  [the longest x1 79.3 us: per_device(): pl.pallas_call(functools.partial(kernel, n, n_pair), out_shape=(jax.Shape...]
where the time goes in v2:
time: 81.6 us; the launch traced here: 81.4 us
  Pallas kernels  81.4 us (100%)
    pallas_call x1, Pallas kernels, per_device(): pl.pallas_call(functools.partial(kernel, n, n_pair), out_shape=(jax.Shape...  79.3 us
    pallas_call x1, Pallas kernels, per_device(): pl.pallas_call(functools.partial(close_kernel, width_cw), out_shape=jax.S...  2.06 us

profile of v2, /device:TPU:1, one launch (start us, length us, event | category | flops | bytes accessed | tf_op | source)
XLA Modules:
  0.0 81.4 jit_solution(6468856733384482732)
XLA Ops:
  0.0 79.3 %shard_map.55 = (f32[10,64,256]{2,1,0:T(8,128)}, f32[10,1,256]{2,1,0:T(1,128)}) custom-call(bf16[8,64,512]{2,1,0:T(8,128)(2,1)} %bitcast.2, bf16[2048,512]{1,0:T(8,128)(2,1)} %metric_hbm.1, s32[8,8]{1,0:T(8,128)} %map_ref.1, s32[4,80]{1,0:T(4,128)} %bitcast.3), custom_call_target="tpu_custom_call" | custom-call | tf_op jit(solution)/shard_map/pallas_call | solution.py:255
  79.3 2.1 %shard_map.56 = f32[10,64,256]{2,1,0:T(8,128)} custom-call(f32[10,64,256]{2,1,0:T(8,128)} %get-tuple-element.7.total_ref, f32[10,1,256]{2,1,0:T(1,128)} %get-tuple-element.8.diag_ref, s32[10]{0:T(128)} %cnt_ref.1), custom_call_target="tpu_custom_call" | custom-call | tf_op jit(solution)/shard_map/pallas_call | solution.py:282

commit v3 on v2

--- a/solution.py
+++ b/solution.py
@@ -12,7 +12,7 @@
 
 def kernel(n, n_pair, b_hbm, metric_hbm, map_ref, dom_ref, out_ref, diag_ref,
            b_raw, b_ref, metric_ref, in_sem, b_all, table, g_send, g_recv, d_own, d_recv,
-           r_s, r_r, l_s, l_r, p_s, p_r, f_s, f_r, g_s, g_r, d_s, d_r):
+           r_s, r_r, l_s, l_r, p_s, p_r, f_s, f_r, g_s, g_r, d_s, d_r, g_far, far_recv, far_send, x_s, x_r, c_s):
     chunks, rows, depth = b_hbm.shape
     pairs, slab, width = out_ref.shape
     slots = dom_ref.shape[0]
@@ -151,6 +151,34 @@
         return remote(g_send.at[lax.rem(z + k, n), p], g_recv.at[k - 1, p],
                       g_s.at[k - 1, p], g_r.at[k - 1, p], (lax.rem(z + k, n), q))
 
+    paired = n == 4
+    is_end = (z == 0) | (z == n - 1)
+    is_mid = jnp.logical_not(is_end)
+    mate = z + 1 - 2 * lax.rem(z, 2)
+
+    def mirrored(i):
+        return jnp.where(z < 2, i, n - 1 - i)
+
+    def near(p):
+        return remote(g_send.at[mate, p], g_recv.at[0, p], g_s.at[0, p], g_r.at[0, p], (mate, q))
+
+    def to_mid(j, p):
+        return remote(g_send.at[mirrored(2 + j), p], far_recv.at[j, p], x_s.at[j, p], x_r.at[j, p], (mate, q))
+
+    def across(j, p):
+        return remote(far_send.at[j, p], g_recv.at[1, p], c_s.at[j, p], g_r.at[1, p], (mirrored(2 + j), q))
+
+    def combine(p, carry):
+        for j in (1, 0):
+            to_mid(j, p).wait_recv()
+            far_send[j, p] = (g_far[j, p] + far_recv[j, p].astype(jnp.float32)).astype(far_send.dtype)
+            across(j, p).start()
+        return carry
+
+    def near_late(p, carry):
+        near(p).start()
+        return carry
+
     def gram(p, carry):
         blocks = []
         for s in range(slots):
@@ -166,11 +194,32 @@
             def _():
                 out_ref[p] = part
 
-            @pl.when(z != d)
-            def _():
-                g_send[d, p] = part.astype(g_send.dtype)
-        for k in range(1, n):
-            gram_copy(k, p).start()
+            if paired:
+                same = (z < 2) == (d < 2)
+
+                @pl.when((z != d) & (is_end | same))
+                def _():
+                    g_send[d, p] = part.astype(g_send.dtype)
+
+                @pl.when(is_mid & jnp.logical_not(same))
+                def _():
+                    g_far[jnp.where(z < 2, d - 2, 1 - d), p] = part
+            else:
+                @pl.when(z != d)
+                def _():
+                    g_send[d, p] = part.astype(g_send.dtype)
+        if paired:
+            @pl.when(is_end)
+            def _():
+                for j in (1, 0):
+                    to_mid(j, p).start()
+
+            @pl.when(is_mid)
+            def _():
+                near(p).start()
+        else:
+            for k in range(1, n):
+                gram_copy(k, p).start()
         return carry
 
     lax.fori_loop(0, pairs, gram, 0)
@@ -180,10 +229,18 @@
 
     for k in range(1, n):
         diag_copy(k).start()
+    if paired:
+        @pl.when(is_end)
+        def _():
+            lax.fori_loop(0, pairs, near_late, 0)
+
+        @pl.when(is_mid)
+        def _():
+            lax.fori_loop(0, pairs, combine, 0)
 
     def add(p, carry):
         total = out_ref[p]
-        for k in range(1, n):
+        for k in range(1, 3 if paired else n):
             gram_copy(k, p).wait_recv()
             total += g_recv[k - 1, p].astype(jnp.float32)
         out_ref[p] = total
@@ -215,8 +272,19 @@
     lax.fori_loop(0, chunks, drain, 0)
 
     def drain_gram(p, carry):
-        for k in range(1, n):
-            gram_copy(k, p).wait_send()
+        if paired:
+            near(p).wait_send()
+            for j in range(2):
+                @pl.when(is_end)
+                def _():
+                    to_mid(j, p).wait_send()
+
+                @pl.when(is_mid)
+                def _():
+                    across(j, p).wait_send()
+        else:
+            for k in range(1, n):
+                gram_copy(k, p).wait_send()
         return carry
 
     lax.fori_loop(0, pairs, drain_gram, 0)
@@ -248,6 +316,7 @@
     slab = width // n
     columns = metric.shape[1]
     chips = n_pair // 2
+    far_pairs = pairs if n == 4 else 1
     vmem = pl.BlockSpec(memory_space=pltpu.VMEM)
     smem = pl.BlockSpec(memory_space=pltpu.SMEM)
     dma = pltpu.SemaphoreType.DMA
@@ -275,6 +344,10 @@
             dma((chips, blocks_dev)), dma((chips, blocks_dev)),
             dma((n - 1, pairs)), dma((n - 1, pairs)),
             dma((n - 1,)), dma((n - 1,)),
+            pltpu.VMEM((2, far_pairs, slab, width), jnp.float32),
+            pltpu.VMEM((2, far_pairs, slab, width), jnp.bfloat16),
+            pltpu.VMEM((2, far_pairs, slab, width), jnp.bfloat16),
+            dma((2, far_pairs)), dma((2, far_pairs)), dma((2, far_pairs)),
         ],
         compiler_params=pltpu.CompilerParams(
             collective_id=0, has_side_effects=True, vmem_limit_bytes=60 * 1024 * 1024),

time: 81.6 us -> 76.8 us (0.941)
  Pallas kernels: 81.4 us -> 76.5 us
    pallas_call x1, Pallas kernels: 79.3 us -> 74.4 us  [per_device(): pl.pallas_call(functools.partial(kernel, n, n_pair), out_shape=(jax.Shape...]
where the time goes in v3:
time: 76.8 us; the launch traced here: 76.5 us
  Pallas kernels  76.5 us (100%)
    pallas_call x1, Pallas kernels, per_device(): pl.pallas_call(functools.partial(kernel, n, n_pair), out_shape=(jax.Shape...  74.4 us
    pallas_call x1, Pallas kernels, per_device(): pl.pallas_call(functools.partial(close_kernel, width_cw), out_shape=jax.S...  2.06 us

profile of v3, /device:TPU:1, one launch (start us, length us, event | category | flops | bytes accessed | tf_op | source)
XLA Modules:
  0.0 76.5 jit_solution(16805577052116796641)
XLA Ops:
  0.0 74.4 %shard_map.55 = (f32[10,64,256]{2,1,0:T(8,128)}, f32[10,1,256]{2,1,0:T(1,128)}) custom-call(bf16[8,64,512]{2,1,0:T(8,128)(2,1)} %bitcast.2, bf16[2048,512]{1,0:T(8,128)(2,1)} %metric_hbm.1, s32[8,8]{1,0:T(8,128)} %map_ref.1, s32[4,80]{1,0:T(4,128)} %bitcast.3), custom_call_target="tpu_custom_call" | custom-call | tf_op jit(solution)/shard_map/pallas_call | solution.py:324
  74.4 2.1 %shard_map.56 = f32[10,64,256]{2,1,0:T(8,128)} custom-call(f32[10,64,256]{2,1,0:T(8,128)} %get-tuple-element.7.total_ref, f32[10,1,256]{2,1,0:T(1,128)} %get-tuple-element.8.diag_ref, s32[10]{0:T(128)} %cnt_ref.1), custom_call_target="tpu_custom_call" | custom-call | tf_op jit(solution)/shard_map/pallas_call | solution.py:355

commit v4 on v3

--- a/solution.py
+++ b/solution.py
@@ -10,7 +10,7 @@
 MESH = pl.DeviceIdType.MESH
 
 
-def kernel(n, n_pair, b_hbm, metric_hbm, map_ref, dom_ref, out_ref, diag_ref,
+def kernel(n, n_pair, split, b_hbm, metric_hbm, map_ref, dom_ref, out_ref, diag_ref,
            b_raw, b_ref, metric_ref, in_sem, b_all, table, g_send, g_recv, d_own, d_recv,
            r_s, r_r, l_s, l_r, p_s, p_r, f_s, f_r, g_s, g_r, d_s, d_r, g_far, far_recv, far_send, x_s, x_r, c_s):
     chunks, rows, depth = b_hbm.shape
@@ -33,8 +33,10 @@
     load_b.start()
     load_metric.start()
     barrier = pltpu.get_barrier_semaphore()
-    for k in range(1, n):
-        pl.semaphore_signal(barrier, inc=1, device_id=(lax.rem(z + k, n), q), device_id_type=MESH)
+    for near_z, there in ((z + 1, has_right), (z - 1, has_left)):
+        @pl.when(there)
+        def _():
+            pl.semaphore_signal(barrier, inc=1, device_id=(near_z, q), device_id_type=MESH)
     for k in range(1, chips):
         pl.semaphore_signal(barrier, inc=1, device_id=(z, chip_at(k)), device_id_type=MESH)
     pl.semaphore_signal(barrier, inc=1, device_id=(z, partner), device_id_type=MESH)
@@ -45,8 +47,8 @@
                    preferred_element_type=jnp.float32)
     load_b.wait()
     for c in range(chunks):
-        b_ref[c] = (b_raw[c].astype(jnp.float32) * keep[c:c + 1, :]).astype(b_ref.dtype)
-    pl.semaphore_wait(barrier, n + chips - 1)
+        b_ref[c] = (b_raw[c].astype(jnp.float32) * keep[c // split:c // split + 1, :]).astype(b_ref.dtype)
+    pl.semaphore_wait(barrier, chips + has_right.astype(jnp.int32) + has_left.astype(jnp.int32))
 
     def remote(src, dst, send, recv, device):
         return pltpu.make_async_remote_copy(
@@ -183,7 +185,9 @@
         blocks = []
         for s in range(slots):
             name = dom_ref[s, q * pairs + p]
-            blocks.append(table[name // chunks, lax.rem(name, chunks)])
+            local = lax.rem(name, chunks // split) * split
+            for t in range(split):
+                blocks.append(table[name // (chunks // split), local + t])
         stack = jnp.concatenate(blocks, axis=0)
         full = lax.dot_general(stack, stack, (((1,), (1,)), ((), ())), preferred_element_type=jnp.float32)
         d_own[p] = jnp.sum(jnp.where(row_of == col_of, full, 0.0), axis=0, keepdims=True)
@@ -314,6 +318,9 @@
     slots = domains.shape[1]
     width = slots * width_cw
     slab = width // n
+    split = 2 if n == 4 else 1
+    chunks = blocks_dev * split
+    chunk_rows = width_cw // split
     columns = metric.shape[1]
     chips = n_pair // 2
     far_pairs = pairs if n == 4 else 1
@@ -322,26 +329,26 @@
     dma = pltpu.SemaphoreType.DMA
     hbm = pl.BlockSpec(memory_space=pl.ANY)
     total, diag = pl.pallas_call(
-        functools.partial(kernel, n, n_pair),
+        functools.partial(kernel, n, n_pair, split),
         out_shape=(jax.ShapeDtypeStruct((pairs, slab, width), jnp.float32),
                    jax.ShapeDtypeStruct((pairs, 1, width), jnp.float32)),
         in_specs=[hbm, hbm, vmem, smem],
         out_specs=(vmem, vmem),
         scratch_shapes=[
-            pltpu.VMEM((blocks_dev, width_cw, aux_dev), jnp.bfloat16),
-            pltpu.VMEM((blocks_dev, width_cw, aux_dev), jnp.bfloat16),
+            pltpu.VMEM((chunks, chunk_rows, aux_dev), jnp.bfloat16),
+            pltpu.VMEM((chunks, chunk_rows, aux_dev), jnp.bfloat16),
             pltpu.VMEM(metric.shape, jnp.bfloat16),
             dma((2,)),
-            pltpu.VMEM((n, blocks_dev, width_cw, aux_dev), jnp.bfloat16),
-            pltpu.VMEM((n_pair, blocks_dev, width_cw, columns), jnp.bfloat16),
+            pltpu.VMEM((n, chunks, chunk_rows, aux_dev), jnp.bfloat16),
+            pltpu.VMEM((n_pair, chunks, chunk_rows, columns), jnp.bfloat16),
             pltpu.VMEM((n, pairs, slab, width), jnp.bfloat16),
             pltpu.VMEM((n - 1, pairs, slab, width), jnp.bfloat16),
             pltpu.VMEM((pairs, 1, width), jnp.float32),
             pltpu.VMEM((n - 1, pairs, 1, width), jnp.float32),
-            dma((n - 1, blocks_dev)), dma((n - 1, blocks_dev)),
-            dma((n - 1, blocks_dev)), dma((n - 1, blocks_dev)),
-            dma((chips, blocks_dev)), dma((chips, blocks_dev)),
-            dma((chips, blocks_dev)), dma((chips, blocks_dev)),
+            dma((n - 1, chunks)), dma((n - 1, chunks)),
+            dma((n - 1, chunks)), dma((n - 1, chunks)),
+            dma((chips, chunks)), dma((chips, chunks)),
+            dma((chips, chunks)), dma((chips, chunks)),
             dma((n - 1, pairs)), dma((n - 1, pairs)),
             dma((n - 1,)), dma((n - 1,)),
             pltpu.VMEM((2, far_pairs, slab, width), jnp.float32),
@@ -351,7 +358,7 @@
         ],
         compiler_params=pltpu.CompilerParams(
             collective_id=0, has_side_effects=True, vmem_limit_bytes=60 * 1024 * 1024),
-    )(b_three.reshape(blocks_dev, width_cw, aux_dev), metric, aux_map, domains.T)
+    )(b_three.reshape(chunks, chunk_rows, aux_dev), metric, aux_map, domains.T)
     return pl.pallas_call(
         functools.partial(close_kernel, width_cw),
         out_shape=jax.ShapeDtypeStruct((pairs, slab, width), jnp.float32),

time: 76.8 us -> 85.3 us (1.11)
  Pallas kernels: 76.5 us -> 84.8 us
    pallas_call x1, Pallas kernels: 74.4 us -> 82.7 us  [per_device(): pl.pallas_call(functools.partial(kernel, n, n_pair, split), out_shape=(ja...]
where the time goes in v4:
time: 85.3 us; the launch traced here: 84.8 us
  Pallas kernels  84.8 us (99%)
    pallas_call x1, Pallas kernels, per_device(): pl.pallas_call(functools.partial(kernel, n, n_pair, split), out_shape=(ja...  82.7 us
    pallas_call x1, Pallas kernels, per_device(): pl.pallas_call(functools.partial(close_kernel, width_cw), out_shape=jax.S...  2.06 us

profile of v4, /device:TPU:1, one launch (start us, length us, event | category | flops | bytes accessed | tf_op | source)
XLA Modules:
  0.0 84.8 jit_solution(8286938917364092052)
XLA Ops:
  0.0 82.7 %shard_map.55 = (f32[10,64,256]{2,1,0:T(8,128)}, f32[10,1,256]{2,1,0:T(1,128)}) custom-call(bf16[16,32,512]{2,1,0:T(8,128)(2,1)} %bitcast.2, bf16[2048,512]{1,0:T(8,128)(2,1)} %metric_hbm.1, s32[8,8]{1,0:T(8,128)} %map_ref.1, s32[4,80]{1,0:T(4,128)} %bitcast.3), custom_call_target="tpu_custom_call" | custom-call | tf_op jit(solution)/shard_map/pallas_call | solution.py:331
  82.7 2.1 %shard_map.56 = f32[10,64,256]{2,1,0:T(8,128)} custom-call(f32[10,64,256]{2,1,0:T(8,128)} %get-tuple-element.7.total_ref, f32[10,1,256]{2,1,0:T(1,128)} %get-tuple-element.8.diag_ref, s32[10]{0:T(128)} %cnt_ref.1), custom_call_target="tpu_custom_call" | custom-call | tf_op jit(solution)/shard_map/pallas_call | solution.py:362

commit v5 on v4

--- a/solution.py
+++ b/solution.py
@@ -12,7 +12,7 @@
 
 def kernel(n, n_pair, split, b_hbm, metric_hbm, map_ref, dom_ref, out_ref, diag_ref,
            b_raw, b_ref, metric_ref, in_sem, b_all, table, g_send, g_recv, d_own, d_recv,
-           r_s, r_r, l_s, l_r, p_s, p_r, f_s, f_r, g_s, g_r, d_s, d_r, g_far, far_recv, far_send, x_s, x_r, c_s):
+           r_s, r_r, l_s, l_r, p_s, p_r, f_s, f_r, g_s, g_r, d_s, d_r, g_far, far_out, far_recv, far_send, late_send, late_recv, x_s, x_r, c_s):
     chunks, rows, depth = b_hbm.shape
     pairs, slab, width = out_ref.shape
     slots = dom_ref.shape[0]
@@ -158,27 +158,36 @@
     is_mid = jnp.logical_not(is_end)
     mate = z + 1 - 2 * lax.rem(z, 2)
 
-    def mirrored(i):
-        return jnp.where(z < 2, i, n - 1 - i)
+    half = width // 2
 
     def near(p):
-        return remote(g_send.at[mate, p], g_recv.at[0, p], g_s.at[0, p], g_r.at[0, p], (mate, q))
-
-    def to_mid(j, p):
-        return remote(g_send.at[mirrored(2 + j), p], far_recv.at[j, p], x_s.at[j, p], x_r.at[j, p], (mate, q))
+        return remote(g_send.at[0, p], g_recv.at[0, p], g_s.at[0, p], g_r.at[0, p], (mate, q))
+
+    def late(p):
+        return remote(late_send.at[p], late_recv.at[p], g_s.at[0, p], g_r.at[0, p], (mate, q))
+
+    def to_mid(p):
+        return remote(far_out.at[p], far_recv.at[p], x_s.at[p], x_r.at[p], (mate, q))
 
     def across(j, p):
-        return remote(far_send.at[j, p], g_recv.at[1, p], c_s.at[j, p], g_r.at[1, p], (mirrored(2 + j), q))
-
-    def combine(p, carry):
-        for j in (1, 0):
-            to_mid(j, p).wait_recv()
-            far_send[j, p] = (g_far[j, p] + far_recv[j, p].astype(jnp.float32)).astype(far_send.dtype)
-            across(j, p).start()
-        return carry
+        return remote(far_send.at[j, p], g_recv.at[1, p], c_s.at[j, p], g_r.at[1, p],
+                      (jnp.where(z < 2, 2, 0) + j, q))
+
+    def combine(low):
+        def one(p, carry):
+            to_mid(p).wait_recv()
+            top = far_recv[p, 0:half].astype(jnp.float32)
+            bottom = far_recv[p, half:width].astype(jnp.float32)
+            parts = (top.T, bottom) if low else (top, bottom.T)
+            value = (g_far[p] + jnp.concatenate(parts, axis=1)).astype(far_send.dtype)
+            for j in ((1, 0) if low else (0, 1)):
+                far_send[j, p] = value[j * slab:(j + 1) * slab]
+                across(j, p).start()
+            return carry
+        lax.fori_loop(0, pairs, one, 0)
 
     def near_late(p, carry):
-        near(p).start()
+        late(p).start()
         return carry
 
     def gram(p, carry):
@@ -198,29 +207,26 @@
             def _():
                 out_ref[p] = part
 
-            if paired:
-                same = (z < 2) == (d < 2)
-
-                @pl.when((z != d) & (is_end | same))
-                def _():
-                    g_send[d, p] = part.astype(g_send.dtype)
-
-                @pl.when(is_mid & jnp.logical_not(same))
-                def _():
-                    g_far[jnp.where(z < 2, d - 2, 1 - d), p] = part
-            else:
+            if not paired:
                 @pl.when(z != d)
                 def _():
                     g_send[d, p] = part.astype(g_send.dtype)
         if paired:
-            @pl.when(is_end)
-            def _():
-                for j in (1, 0):
-                    to_mid(j, p).start()
-
-            @pl.when(is_mid)
-            def _():
-                near(p).start()
+            for end, low in ((0, True), (3, False)):
+                near_cols, far_cols = (slice(0, half), slice(half, width))[::1 if low else -1]
+                mid = 1 if low else 2
+
+                @pl.when(z == end)
+                def _():
+                    far_out[p] = full[:, far_cols].astype(far_out.dtype)
+                    late_send[p] = full[mid * slab:(mid + 1) * slab, near_cols].astype(late_send.dtype)
+                    to_mid(p).start()
+
+                @pl.when(z == mid)
+                def _():
+                    g_far[p] = full[far_cols]
+                    g_send[0, p] = full[end * slab:(end + 1) * slab].astype(g_send.dtype)
+                    near(p).start()
         else:
             for k in range(1, n):
                 gram_copy(k, p).start()
@@ -238,13 +244,31 @@
         def _():
             lax.fori_loop(0, pairs, near_late, 0)
 
-        @pl.when(is_mid)
-        def _():
-            lax.fori_loop(0, pairs, combine, 0)
+        for mid, low in ((1, True), (2, False)):
+            @pl.when(z == mid)
+            def _():
+                combine(low)
 
     def add(p, carry):
+        if paired:
+            remote(g_send.at[0, p], g_recv.at[1, p], g_s.at[0, p], g_r.at[1, p], (mate, q)).wait_recv()
+            total = out_ref[p] + g_recv[1, p].astype(jnp.float32)
+
+            @pl.when(is_end)
+            def _():
+                near(p).wait_recv()
+                out_ref[p] = total + g_recv[0, p].astype(jnp.float32)
+
+            for mid, low in ((1, True), (2, False)):
+                @pl.when(z == mid)
+                def _():
+                    late(p).wait_recv()
+                    parts = (late_recv[p], far_recv[p, mid * slab:(mid + 1) * slab])
+                    whole = jnp.concatenate(parts if low else parts[::-1], axis=1)
+                    out_ref[p] = total + whole.astype(jnp.float32)
+            return carry
         total = out_ref[p]
-        for k in range(1, 3 if paired else n):
+        for k in range(1, n):
             gram_copy(k, p).wait_recv()
             total += g_recv[k - 1, p].astype(jnp.float32)
         out_ref[p] = total
@@ -277,14 +301,15 @@
 
     def drain_gram(p, carry):
         if paired:
-            near(p).wait_send()
-            for j in range(2):
-                @pl.when(is_end)
-                def _():
-                    to_mid(j, p).wait_send()
-
-                @pl.when(is_mid)
-                def _():
+            @pl.when(is_end)
+            def _():
+                late(p).wait_send()
+                to_mid(p).wait_send()
+
+            @pl.when(is_mid)
+            def _():
+                near(p).wait_send()
+                for j in range(2):
                     across(j, p).wait_send()
         else:
             for k in range(1, n):
@@ -318,7 +343,7 @@
     slots = domains.shape[1]
     width = slots * width_cw
     slab = width // n
-    split = 2 if n == 4 else 1
+    split = 1
     chunks = blocks_dev * split
     chunk_rows = width_cw // split
     columns = metric.shape[1]
@@ -351,10 +376,13 @@
             dma((chips, chunks)), dma((chips, chunks)),
             dma((n - 1, pairs)), dma((n - 1, pairs)),
             dma((n - 1,)), dma((n - 1,)),
-            pltpu.VMEM((2, far_pairs, slab, width), jnp.float32),
+            pltpu.VMEM((far_pairs, width // 2, width), jnp.float32),
+            pltpu.VMEM((far_pairs, width, width // 2), jnp.bfloat16),
+            pltpu.VMEM((far_pairs, width, width // 2), jnp.bfloat16),
             pltpu.VMEM((2, far_pairs, slab, width), jnp.bfloat16),
-            pltpu.VMEM((2, far_pairs, slab, width), jnp.bfloat16),
-            dma((2, far_pairs)), dma((2, far_pairs)), dma((2, far_pairs)),
+            pltpu.VMEM((far_pairs, slab, width // 2), jnp.bfloat16),
+            pltpu.VMEM((far_pairs, slab, width // 2), jnp.bfloat16),
+            dma((far_pairs,)), dma((far_pairs,)), dma((2, far_pairs)),
         ],
         compiler_params=pltpu.CompilerParams(
             collective_id=0, has_side_effects=True, vmem_limit_bytes=60 * 1024 * 1024),

time: 85.3 us -> 74 us (0.87)
  Pallas kernels: 84.8 us -> 73.8 us
    pallas_call x1, Pallas kernels: 82.7 us -> 71.8 us  [per_device(): pl.pallas_call(functools.partial(kernel, n, n_pair, split), out_shape=(ja...]
where the time goes in v5:
time: 74 us; the launch traced here: 73.8 us
  Pallas kernels  73.8 us (100%)
    pallas_call x1, Pallas kernels, per_device(): pl.pallas_call(functools.partial(kernel, n, n_pair, split), out_shape=(ja...  71.8 us
    pallas_call x1, Pallas kernels, per_device(): pl.pallas_call(functools.partial(close_kernel, width_cw), out_shape=jax.S...  2.06 us

profile of v5, /device:TPU:1, one launch (start us, length us, event | category | flops | bytes accessed | tf_op | source)
XLA Modules:
  0.0 73.8 jit_solution(4025250417307178423)
XLA Ops:
  0.0 71.8 %shard_map.55 = (f32[10,64,256]{2,1,0:T(8,128)}, f32[10,1,256]{2,1,0:T(1,128)}) custom-call(bf16[8,64,512]{2,1,0:T(8,128)(2,1)} %bitcast.2, bf16[2048,512]{1,0:T(8,128)(2,1)} %metric_hbm.1, s32[8,8]{1,0:T(8,128)} %map_ref.1, s32[4,80]{1,0:T(4,128)} %bitcast.3), custom_call_target="tpu_custom_call" | custom-call | tf_op jit(solution)/shard_map/pallas_call | solution.py:356
  71.8 2.1 %shard_map.56 = f32[10,64,256]{2,1,0:T(8,128)} custom-call(f32[10,64,256]{2,1,0:T(8,128)} %get-tuple-element.7.total_ref, f32[10,1,256]{2,1,0:T(1,128)} %get-tuple-element.8.diag_ref, s32[10]{0:T(128)} %cnt_ref.1), custom_call_target="tpu_custom_call" | custom-call | tf_op jit(solution)/shard_map/pallas_call | solution.py:390

commit v6 on v5

--- a/solution.py
+++ b/solution.py
@@ -119,7 +119,7 @@
         @pl.when(step + 1 < chunks)
         def _():
             own_chunk(step + 1)
-        for h in range(1, n):
+        for h in range(n - 1, 0, -1):
             @pl.when((step + 1 >= h) & (step + 1 - h < chunks))
             def _():
                 relay(h, step + 1 - h)

time: 74 us -> 73.4 us (level)
  no operation moved by 1% of the time
where the time goes in v6:
time: 73.4 us; the launch traced here: 73.2 us
  Pallas kernels  73.2 us (100%)
    pallas_call x1, Pallas kernels, per_device(): pl.pallas_call(functools.partial(kernel, n, n_pair, split), out_shape=(ja...  71.2 us
    pallas_call x1, Pallas kernels, per_device(): pl.pallas_call(functools.partial(close_kernel, width_cw), out_shape=jax.S...  2.06 us

profile of v6, /device:TPU:1, one launch (start us, length us, event | category | flops | bytes accessed | tf_op | source)
XLA Modules:
  0.0 73.2 jit_solution(308942668082816106)
XLA Ops:
  0.0 71.2 %shard_map.55 = (f32[10,64,256]{2,1,0:T(8,128)}, f32[10,1,256]{2,1,0:T(1,128)}) custom-call(bf16[8,64,512]{2,1,0:T(8,128)(2,1)} %bitcast.2, bf16[2048,512]{1,0:T(8,128)(2,1)} %metric_hbm.1, s32[8,8]{1,0:T(8,128)} %map_ref.1, s32[4,80]{1,0:T(4,128)} %bitcast.3), custom_call_target="tpu_custom_call" | custom-call | tf_op jit(solution)/shard_map/pallas_call | solution.py:356
  71.2 2.1 %shard_map.56 = f32[10,64,256]{2,1,0:T(8,128)} custom-call(f32[10,64,256]{2,1,0:T(8,128)} %get-tuple-element.7.total_ref, f32[10,1,256]{2,1,0:T(1,128)} %get-tuple-element.8.diag_ref, s32[10]{0:T(128)} %cnt_ref.1), custom_call_target="tpu_custom_call" | custom-call | tf_op jit(solution)/shard_map/pallas_call | solution.py:390

commit v7 on v6

--- a/solution.py
+++ b/solution.py
@@ -28,9 +28,11 @@
     def chip_at(k):
         return lax.rem(chip + k + chips, chips) * 2 + core
 
-    load_b = pltpu.make_async_copy(b_hbm, b_raw, in_sem.at[0])
+    load_b = pltpu.make_async_copy(b_hbm.at[0], b_raw.at[0], in_sem.at[0])
+    load_rest = pltpu.make_async_copy(b_hbm.at[1:], b_raw.at[1:], in_sem.at[2])
     load_metric = pltpu.make_async_copy(metric_hbm, metric_ref, in_sem.at[1])
     load_b.start()
+    load_rest.start()
     load_metric.start()
     barrier = pltpu.get_barrier_semaphore()
     for near_z, there in ((z + 1, has_right), (z - 1, has_left)):
@@ -45,9 +47,10 @@
     spread_col = lax.broadcasted_iota(jnp.int32, (aux_blocks, depth), 1) // (depth // aux_blocks)
     keep = jnp.dot(map_ref[...].astype(jnp.float32), (spread_row == spread_col).astype(jnp.float32),
                    preferred_element_type=jnp.float32)
+    def mask(c):
+        b_ref[c] = (b_raw[c].astype(jnp.float32) * keep[c // split:c // split + 1, :]).astype(b_ref.dtype)
     load_b.wait()
-    for c in range(chunks):
-        b_ref[c] = (b_raw[c].astype(jnp.float32) * keep[c // split:c // split + 1, :]).astype(b_ref.dtype)
+    mask(0)
     pl.semaphore_wait(barrier, chips + has_right.astype(jnp.int32) + has_left.astype(jnp.int32))
 
     def remote(src, dst, send, recv, device):
@@ -113,6 +116,9 @@
             forward(k, c).start()
 
     own_chunk(0)
+    load_rest.wait()
+    for c in range(1, chunks):
+        mask(c)
     load_metric.wait()
 
     def stage(step, carry):
@@ -363,7 +369,7 @@
             pltpu.VMEM((chunks, chunk_rows, aux_dev), jnp.bfloat16),
             pltpu.VMEM((chunks, chunk_rows, aux_dev), jnp.bfloat16),
             pltpu.VMEM(metric.shape, jnp.bfloat16),
-            dma((2,)),
+            dma((3,)),
             pltpu.VMEM((n, chunks, chunk_rows, aux_dev), jnp.bfloat16),
             pltpu.VMEM((n_pair, chunks, chunk_rows, columns), jnp.bfloat16),
             pltpu.VMEM((n, pairs, slab, width), jnp.bfloat16),

time: 73.4 us -> 73.3 us (level)
  no operation moved by 1% of the time
where the time goes in v7:
time: 73.3 us; the launch traced here: 73.1 us
  Pallas kernels  73.1 us (100%)
    pallas_call x1, Pallas kernels, per_device(): pl.pallas_call(functools.partial(kernel, n, n_pair, split), out_shape=(ja...  71.1 us
    pallas_call x1, Pallas kernels, per_device(): pl.pallas_call(functools.partial(close_kernel, width_cw), out_shape=jax.S...  2.06 us

profile of v7, /device:TPU:1, one launch (start us, length us, event | category | flops | bytes accessed | tf_op | source)
XLA Modules:
  0.0 73.1 jit_solution(17675345337496196336)
XLA Ops:
  0.0 71.1 %shard_map.55 = (f32[10,64,256]{2,1,0:T(8,128)}, f32[10,1,256]{2,1,0:T(1,128)}) custom-call(bf16[8,64,512]{2,1,0:T(8,128)(2,1)} %bitcast.2, bf16[2048,512]{1,0:T(8,128)(2,1)} %metric_hbm.1, s32[8,8]{1,0:T(8,128)} %map_ref.1, s32[4,80]{1,0:T(4,128)} %bitcast.3), custom_call_target="tpu_custom_call" | custom-call | tf_op jit(solution)/shard_map/pallas_call | solution.py:362
  71.1 2.1 %shard_map.56 = f32[10,64,256]{2,1,0:T(8,128)} custom-call(f32[10,64,256]{2,1,0:T(8,128)} %get-tuple-element.7.total_ref, f32[10,1,256]{2,1,0:T(1,128)} %get-tuple-element.8.diag_ref, s32[10]{0:T(128)} %cnt_ref.1), custom_call_target="tpu_custom_call" | custom-call | tf_op jit(solution)/shard_map/pallas_call | solution.py:396
